TPU v7x, 256 devices: a whole 4x4x8 slice. The times are simulated.
256 devices in a mesh: freq: 4 (over y), mx: 8 (over x, core), my: 8 (over z).
Axes of the slice: x: 4, y: 4, z: 8, core: 2. Of those that a mesh axis runs over, the one named last changes fastest.
Arguments:
- adjoint_rhs: float32 [4, 2, 3, 512, 2048], P('freq', None, None, 'mx', 'my'), may hold values from -4 to 6
- state: bfloat16 [4, 2, 3, 512, 2048], P('freq', None, None, 'mx', 'my'), may hold values from -1.5 to 1.5
- density: float32 [512, 2048], P('mx', 'my'), may hold values from 0.85 to 1
- stiffness: float32 [512, 2048], P('mx', 'my'), may hold values from 1.5 to 4
- mass: float32 [512, 2048], P('mx', 'my'), may hold values from 0.2 to 1
- omega: float32 [4], P('freq'), may hold values from 0.15 to 0.45
- send_rows: int32 [64, 2048], P(('mx', 'my')), may hold values from 0 to 16383, as said below
- recv_rows: int32 [64, 2048], P(('mx', 'my')), may hold values from 0 to 16383, as said below
- mortar_weight: float32 [64, 2048], P(('mx', 'my')), may hold values from 0 to 1.5, as said below
Outputs:
- adjoint: float32 [4, 2, 3, 512, 2048], P('freq', None, None, 'mx', 'my')
- filtered_sensitivity: float32 [512, 2048], P('mx', 'my')
Inputs may be any that keep to these rules, and one draw needn't show every extreme that they name: `send_rows`: a local cell of the sending device; slots past the live count of a device pair hold 0. `recv_rows`: a local cell of the receiving device; empty slots hold 0. Live slots of a pair come first, up to 32 of them. `mortar_weight`: zero exactly in empty slots, at least 0.5 in live ones; every receiving device has a source device with all 32 slots live.
All inputs are finite; a program needn't handle non-finite values.
Results may differ from a plain program's by a relative error of at most 0.0003.
Values may be sent and summed in bfloat16 or wider, within the bound.
A program may use at most 64 MiB of HBM per device.

v0:
```python
import jax
import jax.numpy as jnp
from jax import lax
from jax.sharding import PartitionSpec as P

ITERS = 20


def extended(x, sides, width):
    for axis, dim in sides:
        size, length = (lax.axis_size(axis), x.shape[dim])
        up = [(i, (i + 1) % size) for i in range(size - 1)]
        down = [(j, i) for i, j in up]
        last = lax.slice_in_dim(x, length - width, length, axis=dim)
        first = lax.slice_in_dim(x, 0, width, axis=dim)
        before = lax.ppermute(last, axis, up)
        after = lax.ppermute(first, axis, down)
        x = jnp.concatenate([before, x, after], axis=dim)
    return x


def on_device(
    adjoint_rhs, state, density, stiffness, mass, omega, send_rows, recv_rows, mortar_weight
):
    rows_x, rows_y = density.shape
    cells = rows_x * rows_y
    w = omega[0]
    stiff = density**3 * stiffness
    dstiff = 3.0 * density**2 * stiffness
    rmass = density * mass
    sources = send_rows[0]
    targets = recv_rows[0]
    weights = mortar_weight[0]
    mdiag = jnp.zeros((cells,), jnp.float32).at[targets].add(weights).reshape(rows_x, rows_y)
    real_d = 4.4 * stiff + 0.3 + mdiag - w * w * rmass
    imag_d = 0.2 * w * (stiff + rmass)
    den = real_d * real_d + imag_d * imag_d
    rhs = adjoint_rhs.reshape(6, rows_x, rows_y)

    def mortar(field):
        sent = field.reshape(6, cells)[:, sources]
        got = lax.all_to_all(sent, ("mx", "my"), split_axis=1, concat_axis=1, tiled=True)
        added = jnp.zeros((6, cells), jnp.float32).at[:, targets].add(got * weights)
        return added.reshape(6, rows_x, rows_y)

    def sweep(step, field):
        padded = extended(field, (("mx", 1), ("my", 2)), 1)
        beside = (
            padded[:, 2:, 1:-1] + padded[:, :-2, 1:-1] + padded[:, 1:-1, 2:] + padded[:, 1:-1, :-2]
        )
        h = rhs + stiff * beside + mortar(field)
        new_re = (h[:3] * real_d + h[3:] * imag_d) / den
        new_im = (h[3:] * real_d - h[:3] * imag_d) / den
        return jnp.concatenate([new_re, new_im], axis=0)

    field = lax.fori_loop(0, ITERS, sweep, jnp.zeros((6, rows_x, rows_y), jnp.float32))
    state_six = state.reshape(6, rows_x, rows_y)
    state_pad = extended(state_six, (("mx", 1), ("my", 2)), 1).astype(jnp.float32)
    u = state_six.astype(jnp.float32)
    nb = (
        state_pad[:, 2:, 1:-1]
        + state_pad[:, :-2, 1:-1]
        + state_pad[:, 1:-1, 2:]
        + state_pad[:, 1:-1, :-2]
    )
    da = 4.4 * dstiff - w * w * mass
    db = 0.2 * w * (dstiff + mass)
    t_re = da * u[:3] - db * u[3:] - dstiff * nb[:3]
    t_im = da * u[3:] + db * u[:3] - dstiff * nb[3:]
    sens = -jnp.sum(field[:3] * t_re - field[3:] * t_im, axis=0)
    total = lax.psum(sens, "freq")
    weighted = extended(density * total, (("mx", 0), ("my", 1)), 1)
    filt = weighted[1:-1, 1:-1]
    filt = filt + 0.5 * (
        weighted[2:, 1:-1] + weighted[:-2, 1:-1] + weighted[1:-1, 2:] + weighted[1:-1, :-2]
    )
    filt = filt + 0.25 * (
        weighted[2:, 2:] + weighted[:-2, :-2] + weighted[2:, :-2] + weighted[:-2, 2:]
    )
    return (field.reshape(1, 2, 3, rows_x, rows_y), filt / (4.0 * density))


def solution(mesh):
    return jax.shard_map(
        on_device,
        mesh=mesh,
        in_specs=(
            P("freq", None, None, "mx", "my"),
            P("freq", None, None, "mx", "my"),
            P("mx", "my"),
            P("mx", "my"),
            P("mx", "my"),
            P("freq"),
            P(("mx", "my"), None),
            P(("mx", "my"), None),
            P(("mx", "my"), None),
        ),
        out_specs=(P("freq", None, None, "mx", "my"), P("mx", "my")),
        check_vma=False,
    )
```

profile of v0, /device:TPU:98, one launch (start us, length us, event | category | flops | bytes accessed | tf_op | source)
XLA Modules:
  0.0 1374.9 jit_solution(1580240488645792618)
XLA Ops:
  13.7 11.6 scatter_custom_fusion.1
  41.8 1255.3 %while.10 = (s32[]{:T(128)}, f32[6,64,256]{2,1,0:T(8,128)S(1)}, f32[64,256]{1,0:T(8,128)S(1)}, f32[6,64,256]{2,1,0:T(8,128)}, s32[2048]{0:T(1024)}, /*index=5*/s...) while((s32[]{:T(128)}, f32[6,64,256]{2,1,0:T(8,128)S(1)}, ...), condition=%wide.region_3.0_spmd, body=%wide.region_1.0_spmd.sunk | while | flops 2109442 | bytes 9095261 | solution.py:56
  46.6 8.8 gather_fusion
  56.7 11.4 all-to-all-start
  83.9 15.2 %scatter_custom_fusion.7 = f32[6,16384]{0,1:T(8,128)} fusion(s32[2048]{0:T(1024)S(1)} %bitcast.65, f32[2048,6]{1,0:T(8,128)S(1)} %copy.34, f32[]{:T(128)} %constant.21.clone.1..sunk), kind=kCustom, calls=%fused_computation.3.clone.1 | custom fusion | flops 12288 | bytes 393220 | tf_op jit(solution)/shard_map/while/body/eval_jaxpr/scatter-add | solution.py:43
  109.8 8.8 gather_fusion
  119.9 10.9 all-to-all-start
  146.7 15.2 %scatter_custom_fusion.7 = f32[6,16384]{0,1:T(8,128)} fusion(s32[2048]{0:T(1024)S(1)} %bitcast.65, f32[2048,6]{1,0:T(8,128)S(1)} %copy.34, f32[]{:T(128)} %constant.21.clone.1..sunk), kind=kCustom, calls=%fused_computation.3.clone.1 | custom fusion | flops 12288 | bytes 393220 | tf_op jit(solution)/shard_map/while/body/eval_jaxpr/scatter-add | solution.py:43
  172.5 8.8 gather_fusion
  182.6 10.9 all-to-all-start
  209.4 15.2 %scatter_custom_fusion.7 = f32[6,16384]{0,1:T(8,128)} fusion(s32[2048]{0:T(1024)S(1)} %bitcast.65, f32[2048,6]{1,0:T(8,128)S(1)} %copy.34, f32[]{:T(128)} %constant.21.clone.1..sunk), kind=kCustom, calls=%fused_computation.3.clone.1 | custom fusion | flops 12288 | bytes 393220 | tf_op jit(solution)/shard_map/while/body/eval_jaxpr/scatter-add | solution.py:43
  235.3 8.8 gather_fusion
  245.4 10.9 all-to-all-start
  272.1 15.2 %scatter_custom_fusion.7 = f32[6,16384]{0,1:T(8,128)} fusion(s32[2048]{0:T(1024)S(1)} %bitcast.65, f32[2048,6]{1,0:T(8,128)S(1)} %copy.34, f32[]{:T(128)} %constant.21.clone.1..sunk), kind=kCustom, calls=%fused_computation.3.clone.1 | custom fusion | flops 12288 | bytes 393220 | tf_op jit(solution)/shard_map/while/body/eval_jaxpr/scatter-add | solution.py:43
  298.0 8.8 gather_fusion
  308.1 10.9 all-to-all-start
  334.9 15.2 %scatter_custom_fusion.7 = f32[6,16384]{0,1:T(8,128)} fusion(s32[2048]{0:T(1024)S(1)} %bitcast.65, f32[2048,6]{1,0:T(8,128)S(1)} %copy.34, f32[]{:T(128)} %constant.21.clone.1..sunk), kind=kCustom, calls=%fused_computation.3.clone.1 | custom fusion | flops 12288 | bytes 393220 | tf_op jit(solution)/shard_map/while/body/eval_jaxpr/scatter-add | solution.py:43
  370.8 10.9 all-to-all-start
  397.6 15.2 %scatter_custom_fusion.7 = f32[6,16384]{0,1:T(8,128)} fusion(s32[2048]{0:T(1024)S(1)} %bitcast.65, f32[2048,6]{1,0:T(8,128)S(1)} %copy.34, f32[]{:T(128)} %constant.21.clone.1..sunk), kind=kCustom, calls=%fused_computation.3.clone.1 | custom fusion | flops 12288 | bytes 393220 | tf_op jit(solution)/shard_map/while/body/eval_jaxpr/scatter-add | solution.py:43
  433.6 10.9 all-to-all-start
  460.4 15.2 %scatter_custom_fusion.7 = f32[6,16384]{0,1:T(8,128)} fusion(s32[2048]{0:T(1024)S(1)} %bitcast.65, f32[2048,6]{1,0:T(8,128)S(1)} %copy.34, f32[]{:T(128)} %constant.21.clone.1..sunk), kind=kCustom, calls=%fused_computation.3.clone.1 | custom fusion | flops 12288 | bytes 393220 | tf_op jit(solution)/shard_map/while/body/eval_jaxpr/scatter-add | solution.py:43
  496.3 10.9 all-to-all-start
  523.1 15.2 %scatter_custom_fusion.7 = f32[6,16384]{0,1:T(8,128)} fusion(s32[2048]{0:T(1024)S(1)} %bitcast.65, f32[2048,6]{1,0:T(8,128)S(1)} %copy.34, f32[]{:T(128)} %constant.21.clone.1..sunk), kind=kCustom, calls=%fused_computation.3.clone.1 | custom fusion | flops 12288 | bytes 393220 | tf_op jit(solution)/shard_map/while/body/eval_jaxpr/scatter-add | solution.py:43
  559.1 10.9 all-to-all-start
  585.8 15.2 %scatter_custom_fusion.7 = f32[6,16384]{0,1:T(8,128)} fusion(s32[2048]{0:T(1024)S(1)} %bitcast.65, f32[2048,6]{1,0:T(8,128)S(1)} %copy.34, f32[]{:T(128)} %constant.21.clone.1..sunk), kind=kCustom, calls=%fused_computation.3.clone.1 | custom fusion | flops 12288 | bytes 393220 | tf_op jit(solution)/shard_map/while/body/eval_jaxpr/scatter-add | solution.py:43
  621.8 10.9 all-to-all-start
  648.6 15.2 %scatter_custom_fusion.7 = f32[6,16384]{0,1:T(8,128)} fusion(s32[2048]{0:T(1024)S(1)} %bitcast.65, f32[2048,6]{1,0:T(8,128)S(1)} %copy.34, f32[]{:T(128)} %constant.21.clone.1..sunk), kind=kCustom, calls=%fused_computation.3.clone.1 | custom fusion | flops 12288 | bytes 393220 | tf_op jit(solution)/shard_map/while/body/eval_jaxpr/scatter-add | solution.py:43
  684.5 10.9 all-to-all-start
  711.3 15.2 %scatter_custom_fusion.7 = f32[6,16384]{0,1:T(8,128)} fusion(s32[2048]{0:T(1024)S(1)} %bitcast.65, f32[2048,6]{1,0:T(8,128)S(1)} %copy.34, f32[]{:T(128)} %constant.21.clone.1..sunk), kind=kCustom, calls=%fused_computation.3.clone.1 | custom fusion | flops 12288 | bytes 393220 | tf_op jit(solution)/shard_map/while/body/eval_jaxpr/scatter-add | solution.py:43
  747.3 10.9 all-to-all-start
  774.1 15.2 %scatter_custom_fusion.7 = f32[6,16384]{0,1:T(8,128)} fusion(s32[2048]{0:T(1024)S(1)} %bitcast.65, f32[2048,6]{1,0:T(8,128)S(1)} %copy.34, f32[]{:T(128)} %constant.21.clone.1..sunk), kind=kCustom, calls=%fused_computation.3.clone.1 | custom fusion | flops 12288 | bytes 393220 | tf_op jit(solution)/shard_map/while/body/eval_jaxpr/scatter-add | solution.py:43
  810.0 10.9 all-to-all-start
  836.8 15.2 %scatter_custom_fusion.7 = f32[6,16384]{0,1:T(8,128)} fusion(s32[2048]{0:T(1024)S(1)} %bitcast.65, f32[2048,6]{1,0:T(8,128)S(1)} %copy.34, f32[]{:T(128)} %constant.21.clone.1..sunk), kind=kCustom, calls=%fused_computation.3.clone.1 | custom fusion | flops 12288 | bytes 393220 | tf_op jit(solution)/shard_map/while/body/eval_jaxpr/scatter-add | solution.py:43
  872.8 10.9 all-to-all-start
  899.5 15.2 %scatter_custom_fusion.7 = f32[6,16384]{0,1:T(8,128)} fusion(s32[2048]{0:T(1024)S(1)} %bitcast.65, f32[2048,6]{1,0:T(8,128)S(1)} %copy.34, f32[]{:T(128)} %constant.21.clone.1..sunk), kind=kCustom, calls=%fused_computation.3.clone.1 | custom fusion | flops 12288 | bytes 393220 | tf_op jit(solution)/shard_map/while/body/eval_jaxpr/scatter-add | solution.py:43
  935.5 10.9 all-to-all-start
  962.3 15.2 %scatter_custom_fusion.7 = f32[6,16384]{0,1:T(8,128)} fusion(s32[2048]{0:T(1024)S(1)} %bitcast.65, f32[2048,6]{1,0:T(8,128)S(1)} %copy.34, f32[]{:T(128)} %constant.21.clone.1..sunk), kind=kCustom, calls=%fused_computation.3.clone.1 | custom fusion | flops 12288 | bytes 393220 | tf_op jit(solution)/shard_map/while/body/eval_jaxpr/scatter-add | solution.py:43
  998.2 10.9 all-to-all-start
  1025.0 15.2 %scatter_custom_fusion.7 = f32[6,16384]{0,1:T(8,128)} fusion(s32[2048]{0:T(1024)S(1)} %bitcast.65, f32[2048,6]{1,0:T(8,128)S(1)} %copy.34, f32[]{:T(128)} %constant.21.clone.1..sunk), kind=kCustom, calls=%fused_computation.3.clone.1 | custom fusion | flops 12288 | bytes 393220 | tf_op jit(solution)/shard_map/while/body/eval_jaxpr/scatter-add | solution.py:43
  1061.0 10.9 all-to-all-start
  1087.8 15.2 %scatter_custom_fusion.7 = f32[6,16384]{0,1:T(8,128)} fusion(s32[2048]{0:T(1024)S(1)} %bitcast.65, f32[2048,6]{1,0:T(8,128)S(1)} %copy.34, f32[]{:T(128)} %constant.21.clone.1..sunk), kind=kCustom, calls=%fused_computation.3.clone.1 | custom fusion | flops 12288 | bytes 393220 | tf_op jit(solution)/shard_map/while/body/eval_jaxpr/scatter-add | solution.py:43
  1123.7 10.9 all-to-all-start
  1150.5 15.2 %scatter_custom_fusion.7 = f32[6,16384]{0,1:T(8,128)} fusion(s32[2048]{0:T(1024)S(1)} %bitcast.65, f32[2048,6]{1,0:T(8,128)S(1)} %copy.34, f32[]{:T(128)} %constant.21.clone.1..sunk), kind=kCustom, calls=%fused_computation.3.clone.1 | custom fusion | flops 12288 | bytes 393220 | tf_op jit(solution)/shard_map/while/body/eval_jaxpr/scatter-add | solution.py:43
  1186.5 10.9 all-to-all-start
  1213.2 15.2 %scatter_custom_fusion.7 = f32[6,16384]{0,1:T(8,128)} fusion(s32[2048]{0:T(1024)S(1)} %bitcast.65, f32[2048,6]{1,0:T(8,128)S(1)} %copy.34, f32[]{:T(128)} %constant.21.clone.1..sunk), kind=kCustom, calls=%fused_computation.3.clone.1 | custom fusion | flops 12288 | bytes 393220 | tf_op jit(solution)/shard_map/while/body/eval_jaxpr/scatter-add | solution.py:43
  1249.2 10.9 all-to-all-start
  1276.0 15.2 %scatter_custom_fusion.7 = f32[6,16384]{0,1:T(8,128)} fusion(s32[2048]{0:T(1024)S(1)} %bitcast.65, f32[2048,6]{1,0:T(8,128)S(1)} %copy.34, f32[]{:T(128)} %constant.21.clone.1..sunk), kind=kCustom, calls=%fused_computation.3.clone.1 | custom fusion | flops 12288 | bytes 393220 | tf_op jit(solution)/shard_map/while/body/eval_jaxpr/scatter-add | solution.py:43
  1299.1 48.6 %all-reduce.2.cloned.1.call-done = f32[64,256]{1,0:T(8,128)} async-done(((f32[64,256]{1,0:T(8,128)}), f32[64,256]{1,0:T(8,128)}) %all-reduce.2.cloned.1.call-update) | async-done | bytes 65552 | tf_op jit(solution)/shard_map/psum | solution.py:71
  (798 shorter events, 727.4 us)
Async XLA Ops:
  7.2 1340.5 %all-reduce.2.cloned.1.call-start = ((), (), s32[]{:S(2)}) async-start(), calls=%async_computation.1 | async-start | bytes 131072 | tf_op jit(solution)/shard_map/psum | solution.py:71
  56.7 25.2 %all-to-all-start = ((f32[64,1,192]{2,1,0:T(1,128)}), f32[64,1,192]{2,1,0:T(1,128)S(1)}, u32[]{:S(2)}, u32[]{:S(2)}) async-start(f32[64,1,192]{2,1,0:T(1,128)} %reshape.136), calls=%async_computation | async-start | bytes 131072 | tf_op jit(solution)/shard_map/while/body/eval_jaxpr/all_to_all | solution.py:42
  75.4 29.1 %collective-permute-start.2 = (f32[6,66,1]{2,1,0:T(8,128)S(1)}, f32[6,66,1]{2,1,0:T(8,128)S(1)}, u32[]{:S(2)}, u32[]{:S(2)}) collective-permute-start(f32[6,66,1]{2,1,0:T(8,128)S(1)} %get-tuple-element.180), channel_id=1, source_target_pairs={{0,1},{1,2},{2,3},{3,4},{4,5},{5,6},{6,7},{8,9},{9,10},{10,11},{11... | collective-permute-start | bytes 4760 | tf_op jit(solution)/shard_map/while/body/eval_jaxpr/ppermute | solution.py:16
  80.0 24.5 %collective-permute-start.3 = (f32[6,66,1]{2,1,0:T(8,128)S(1)}, f32[6,66,1]{2,1,0:T(8,128)S(1)}, u32[]{:S(2)}, u32[]{:S(2)}) collective-permute-start(f32[6,66,1]{2,1,0:T(8,128)S(1)} %get-tuple-element.181), channel_id=1, source_target_pairs={{1,0},{2,1},{3,2},{4,3},{5,4},{6,5},{7,6},{9,8},{10,9},{11,10},{12... | collective-permute-start | bytes 4760 | tf_op jit(solution)/shard_map/while/body/eval_jaxpr/ppermute | solution.py:17
  119.9 24.8 %all-to-all-start = ((f32[64,1,192]{2,1,0:T(1,128)}), f32[64,1,192]{2,1,0:T(1,128)S(1)}, u32[]{:S(2)}, u32[]{:S(2)}) async-start(f32[64,1,192]{2,1,0:T(1,128)} %reshape.136), calls=%async_computation | async-start | bytes 131072 | tf_op jit(solution)/shard_map/while/body/eval_jaxpr/all_to_all | solution.py:42
  138.1 29.1 %collective-permute-start.2 = (f32[6,66,1]{2,1,0:T(8,128)S(1)}, f32[6,66,1]{2,1,0:T(8,128)S(1)}, u32[]{:S(2)}, u32[]{:S(2)}) collective-permute-start(f32[6,66,1]{2,1,0:T(8,128)S(1)} %get-tuple-element.180), channel_id=1, source_target_pairs={{0,1},{1,2},{2,3},{3,4},{4,5},{5,6},{6,7},{8,9},{9,10},{10,11},{11... | collective-permute-start | bytes 4760 | tf_op jit(solution)/shard_map/while/body/eval_jaxpr/ppermute | solution.py:16
  142.7 24.5 %collective-permute-start.3 = (f32[6,66,1]{2,1,0:T(8,128)S(1)}, f32[6,66,1]{2,1,0:T(8,128)S(1)}, u32[]{:S(2)}, u32[]{:S(2)}) collective-permute-start(f32[6,66,1]{2,1,0:T(8,128)S(1)} %get-tuple-element.181), channel_id=1, source_target_pairs={{1,0},{2,1},{3,2},{4,3},{5,4},{6,5},{7,6},{9,8},{10,9},{11,10},{12... | collective-permute-start | bytes 4760 | tf_op jit(solution)/shard_map/while/body/eval_jaxpr/ppermute | solution.py:17
  182.6 24.8 %all-to-all-start = ((f32[64,1,192]{2,1,0:T(1,128)}), f32[64,1,192]{2,1,0:T(1,128)S(1)}, u32[]{:S(2)}, u32[]{:S(2)}) async-start(f32[64,1,192]{2,1,0:T(1,128)} %reshape.136), calls=%async_computation | async-start | bytes 131072 | tf_op jit(solution)/shard_map/while/body/eval_jaxpr/all_to_all | solution.py:42
  200.9 29.1 %collective-permute-start.2 = (f32[6,66,1]{2,1,0:T(8,128)S(1)}, f32[6,66,1]{2,1,0:T(8,128)S(1)}, u32[]{:S(2)}, u32[]{:S(2)}) collective-permute-start(f32[6,66,1]{2,1,0:T(8,128)S(1)} %get-tuple-element.180), channel_id=1, source_target_pairs={{0,1},{1,2},{2,3},{3,4},{4,5},{5,6},{6,7},{8,9},{9,10},{10,11},{11... | collective-permute-start | bytes 4760 | tf_op jit(solution)/shard_map/while/body/eval_jaxpr/ppermute | solution.py:16
  205.5 24.5 %collective-permute-start.3 = (f32[6,66,1]{2,1,0:T(8,128)S(1)}, f32[6,66,1]{2,1,0:T(8,128)S(1)}, u32[]{:S(2)}, u32[]{:S(2)}) collective-permute-start(f32[6,66,1]{2,1,0:T(8,128)S(1)} %get-tuple-element.181), channel_id=1, source_target_pairs={{1,0},{2,1},{3,2},{4,3},{5,4},{6,5},{7,6},{9,8},{10,9},{11,10},{12... | collective-permute-start | bytes 4760 | tf_op jit(solution)/shard_map/while/body/eval_jaxpr/ppermute | solution.py:17
  245.4 24.8 %all-to-all-start = ((f32[64,1,192]{2,1,0:T(1,128)}), f32[64,1,192]{2,1,0:T(1,128)S(1)}, u32[]{:S(2)}, u32[]{:S(2)}) async-start(f32[64,1,192]{2,1,0:T(1,128)} %reshape.136), calls=%async_computation | async-start | bytes 131072 | tf_op jit(solution)/shard_map/while/body/eval_jaxpr/all_to_all | solution.py:42
  263.6 29.1 %collective-permute-start.2 = (f32[6,66,1]{2,1,0:T(8,128)S(1)}, f32[6,66,1]{2,1,0:T(8,128)S(1)}, u32[]{:S(2)}, u32[]{:S(2)}) collective-permute-start(f32[6,66,1]{2,1,0:T(8,128)S(1)} %get-tuple-element.180), channel_id=1, source_target_pairs={{0,1},{1,2},{2,3},{3,4},{4,5},{5,6},{6,7},{8,9},{9,10},{10,11},{11... | collective-permute-start | bytes 4760 | tf_op jit(solution)/shard_map/while/body/eval_jaxpr/ppermute | solution.py:16
  268.2 24.5 %collective-permute-start.3 = (f32[6,66,1]{2,1,0:T(8,128)S(1)}, f32[6,66,1]{2,1,0:T(8,128)S(1)}, u32[]{:S(2)}, u32[]{:S(2)}) collective-permute-start(f32[6,66,1]{2,1,0:T(8,128)S(1)} %get-tuple-element.181), channel_id=1, source_target_pairs={{1,0},{2,1},{3,2},{4,3},{5,4},{6,5},{7,6},{9,8},{10,9},{11,10},{12... | collective-permute-start | bytes 4760 | tf_op jit(solution)/shard_map/while/body/eval_jaxpr/ppermute | solution.py:17
  308.1 24.8 %all-to-all-start = ((f32[64,1,192]{2,1,0:T(1,128)}), f32[64,1,192]{2,1,0:T(1,128)S(1)}, u32[]{:S(2)}, u32[]{:S(2)}) async-start(f32[64,1,192]{2,1,0:T(1,128)} %reshape.136), calls=%async_computation | async-start | bytes 131072 | tf_op jit(solution)/shard_map/while/body/eval_jaxpr/all_to_all | solution.py:42
  326.4 29.1 %collective-permute-start.2 = (f32[6,66,1]{2,1,0:T(8,128)S(1)}, f32[6,66,1]{2,1,0:T(8,128)S(1)}, u32[]{:S(2)}, u32[]{:S(2)}) collective-permute-start(f32[6,66,1]{2,1,0:T(8,128)S(1)} %get-tuple-element.180), channel_id=1, source_target_pairs={{0,1},{1,2},{2,3},{3,4},{4,5},{5,6},{6,7},{8,9},{9,10},{10,11},{11... | collective-permute-start | bytes 4760 | tf_op jit(solution)/shard_map/while/body/eval_jaxpr/ppermute | solution.py:16
  330.9 24.5 %collective-permute-start.3 = (f32[6,66,1]{2,1,0:T(8,128)S(1)}, f32[6,66,1]{2,1,0:T(8,128)S(1)}, u32[]{:S(2)}, u32[]{:S(2)}) collective-permute-start(f32[6,66,1]{2,1,0:T(8,128)S(1)} %get-tuple-element.181), channel_id=1, source_target_pairs={{1,0},{2,1},{3,2},{4,3},{5,4},{6,5},{7,6},{9,8},{10,9},{11,10},{12... | collective-permute-start | bytes 4760 | tf_op jit(solution)/shard_map/while/body/eval_jaxpr/ppermute | solution.py:17
  370.8 24.8 %all-to-all-start = ((f32[64,1,192]{2,1,0:T(1,128)}), f32[64,1,192]{2,1,0:T(1,128)S(1)}, u32[]{:S(2)}, u32[]{:S(2)}) async-start(f32[64,1,192]{2,1,0:T(1,128)} %reshape.136), calls=%async_computation | async-start | bytes 131072 | tf_op jit(solution)/shard_map/while/body/eval_jaxpr/all_to_all | solution.py:42
  389.1 29.1 %collective-permute-start.2 = (f32[6,66,1]{2,1,0:T(8,128)S(1)}, f32[6,66,1]{2,1,0:T(8,128)S(1)}, u32[]{:S(2)}, u32[]{:S(2)}) collective-permute-start(f32[6,66,1]{2,1,0:T(8,128)S(1)} %get-tuple-element.180), channel_id=1, source_target_pairs={{0,1},{1,2},{2,3},{3,4},{4,5},{5,6},{6,7},{8,9},{9,10},{10,11},{11... | collective-permute-start | bytes 4760 | tf_op jit(solution)/shard_map/while/body/eval_jaxpr/ppermute | solution.py:16
  393.7 24.5 %collective-permute-start.3 = (f32[6,66,1]{2,1,0:T(8,128)S(1)}, f32[6,66,1]{2,1,0:T(8,128)S(1)}, u32[]{:S(2)}, u32[]{:S(2)}) collective-permute-start(f32[6,66,1]{2,1,0:T(8,128)S(1)} %get-tuple-element.181), channel_id=1, source_target_pairs={{1,0},{2,1},{3,2},{4,3},{5,4},{6,5},{7,6},{9,8},{10,9},{11,10},{12... | collective-permute-start | bytes 4760 | tf_op jit(solution)/shard_map/while/body/eval_jaxpr/ppermute | solution.py:17
  433.6 24.8 %all-to-all-start = ((f32[64,1,192]{2,1,0:T(1,128)}), f32[64,1,192]{2,1,0:T(1,128)S(1)}, u32[]{:S(2)}, u32[]{:S(2)}) async-start(f32[64,1,192]{2,1,0:T(1,128)} %reshape.136), calls=%async_computation | async-start | bytes 131072 | tf_op jit(solution)/shard_map/while/body/eval_jaxpr/all_to_all | solution.py:42
  451.8 29.1 %collective-permute-start.2 = (f32[6,66,1]{2,1,0:T(8,128)S(1)}, f32[6,66,1]{2,1,0:T(8,128)S(1)}, u32[]{:S(2)}, u32[]{:S(2)}) collective-permute-start(f32[6,66,1]{2,1,0:T(8,128)S(1)} %get-tuple-element.180), channel_id=1, source_target_pairs={{0,1},{1,2},{2,3},{3,4},{4,5},{5,6},{6,7},{8,9},{9,10},{10,11},{11... | collective-permute-start | bytes 4760 | tf_op jit(solution)/shard_map/while/body/eval_jaxpr/ppermute | solution.py:16
  456.4 24.5 %collective-permute-start.3 = (f32[6,66,1]{2,1,0:T(8,128)S(1)}, f32[6,66,1]{2,1,0:T(8,128)S(1)}, u32[]{:S(2)}, u32[]{:S(2)}) collective-permute-start(f32[6,66,1]{2,1,0:T(8,128)S(1)} %get-tuple-element.181), channel_id=1, source_target_pairs={{1,0},{2,1},{3,2},{4,3},{5,4},{6,5},{7,6},{9,8},{10,9},{11,10},{12... | collective-permute-start | bytes 4760 | tf_op jit(solution)/shard_map/while/body/eval_jaxpr/ppermute | solution.py:17
  496.3 24.8 %all-to-all-start = ((f32[64,1,192]{2,1,0:T(1,128)}), f32[64,1,192]{2,1,0:T(1,128)S(1)}, u32[]{:S(2)}, u32[]{:S(2)}) async-start(f32[64,1,192]{2,1,0:T(1,128)} %reshape.136), calls=%async_computation | async-start | bytes 131072 | tf_op jit(solution)/shard_map/while/body/eval_jaxpr/all_to_all | solution.py:42
  514.6 29.1 %collective-permute-start.2 = (f32[6,66,1]{2,1,0:T(8,128)S(1)}, f32[6,66,1]{2,1,0:T(8,128)S(1)}, u32[]{:S(2)}, u32[]{:S(2)}) collective-permute-start(f32[6,66,1]{2,1,0:T(8,128)S(1)} %get-tuple-element.180), channel_id=1, source_target_pairs={{0,1},{1,2},{2,3},{3,4},{4,5},{5,6},{6,7},{8,9},{9,10},{10,11},{11... | collective-permute-start | bytes 4760 | tf_op jit(solution)/shard_map/while/body/eval_jaxpr/ppermute | solution.py:16
  559.1 24.8 %all-to-all-start = ((f32[64,1,192]{2,1,0:T(1,128)}), f32[64,1,192]{2,1,0:T(1,128)S(1)}, u32[]{:S(2)}, u32[]{:S(2)}) async-start(f32[64,1,192]{2,1,0:T(1,128)} %reshape.136), calls=%async_computation | async-start | bytes 131072 | tf_op jit(solution)/shard_map/while/body/eval_jaxpr/all_to_all | solution.py:42
  577.3 29.1 %collective-permute-start.2 = (f32[6,66,1]{2,1,0:T(8,128)S(1)}, f32[6,66,1]{2,1,0:T(8,128)S(1)}, u32[]{:S(2)}, u32[]{:S(2)}) collective-permute-start(f32[6,66,1]{2,1,0:T(8,128)S(1)} %get-tuple-element.180), channel_id=1, source_target_pairs={{0,1},{1,2},{2,3},{3,4},{4,5},{5,6},{6,7},{8,9},{9,10},{10,11},{11... | collective-permute-start | bytes 4760 | tf_op jit(solution)/shard_map/while/body/eval_jaxpr/ppermute | solution.py:16
  621.8 24.8 %all-to-all-start = ((f32[64,1,192]{2,1,0:T(1,128)}), f32[64,1,192]{2,1,0:T(1,128)S(1)}, u32[]{:S(2)}, u32[]{:S(2)}) async-start(f32[64,1,192]{2,1,0:T(1,128)} %reshape.136), calls=%async_computation | async-start | bytes 131072 | tf_op jit(solution)/shard_map/while/body/eval_jaxpr/all_to_all | solution.py:42
  640.1 29.1 %collective-permute-start.2 = (f32[6,66,1]{2,1,0:T(8,128)S(1)}, f32[6,66,1]{2,1,0:T(8,128)S(1)}, u32[]{:S(2)}, u32[]{:S(2)}) collective-permute-start(f32[6,66,1]{2,1,0:T(8,128)S(1)} %get-tuple-element.180), channel_id=1, source_target_pairs={{0,1},{1,2},{2,3},{3,4},{4,5},{5,6},{6,7},{8,9},{9,10},{10,11},{11... | collective-permute-start | bytes 4760 | tf_op jit(solution)/shard_map/while/body/eval_jaxpr/ppermute | solution.py:16
  684.5 24.8 %all-to-all-start = ((f32[64,1,192]{2,1,0:T(1,128)}), f32[64,1,192]{2,1,0:T(1,128)S(1)}, u32[]{:S(2)}, u32[]{:S(2)}) async-start(f32[64,1,192]{2,1,0:T(1,128)} %reshape.136), calls=%async_computation | async-start | bytes 131072 | tf_op jit(solution)/shard_map/while/body/eval_jaxpr/all_to_all | solution.py:42
  702.8 29.1 %collective-permute-start.2 = (f32[6,66,1]{2,1,0:T(8,128)S(1)}, f32[6,66,1]{2,1,0:T(8,128)S(1)}, u32[]{:S(2)}, u32[]{:S(2)}) collective-permute-start(f32[6,66,1]{2,1,0:T(8,128)S(1)} %get-tuple-element.180), channel_id=1, source_target_pairs={{0,1},{1,2},{2,3},{3,4},{4,5},{5,6},{6,7},{8,9},{9,10},{10,11},{11... | collective-permute-start | bytes 4760 | tf_op jit(solution)/shard_map/while/body/eval_jaxpr/ppermute | solution.py:16
  747.3 24.8 %all-to-all-start = ((f32[64,1,192]{2,1,0:T(1,128)}), f32[64,1,192]{2,1,0:T(1,128)S(1)}, u32[]{:S(2)}, u32[]{:S(2)}) async-start(f32[64,1,192]{2,1,0:T(1,128)} %reshape.136), calls=%async_computation | async-start | bytes 131072 | tf_op jit(solution)/shard_map/while/body/eval_jaxpr/all_to_all | solution.py:42
  765.5 29.1 %collective-permute-start.2 = (f32[6,66,1]{2,1,0:T(8,128)S(1)}, f32[6,66,1]{2,1,0:T(8,128)S(1)}, u32[]{:S(2)}, u32[]{:S(2)}) collective-permute-start(f32[6,66,1]{2,1,0:T(8,128)S(1)} %get-tuple-element.180), channel_id=1, source_target_pairs={{0,1},{1,2},{2,3},{3,4},{4,5},{5,6},{6,7},{8,9},{9,10},{10,11},{11... | collective-permute-start | bytes 4760 | tf_op jit(solution)/shard_map/while/body/eval_jaxpr/ppermute | solution.py:16
  810.0 24.8 %all-to-all-start = ((f32[64,1,192]{2,1,0:T(1,128)}), f32[64,1,192]{2,1,0:T(1,128)S(1)}, u32[]{:S(2)}, u32[]{:S(2)}) async-start(f32[64,1,192]{2,1,0:T(1,128)} %reshape.136), calls=%async_computation | async-start | bytes 131072 | tf_op jit(solution)/shard_map/while/body/eval_jaxpr/all_to_all | solution.py:42
  828.3 29.1 %collective-permute-start.2 = (f32[6,66,1]{2,1,0:T(8,128)S(1)}, f32[6,66,1]{2,1,0:T(8,128)S(1)}, u32[]{:S(2)}, u32[]{:S(2)}) collective-permute-start(f32[6,66,1]{2,1,0:T(8,128)S(1)} %get-tuple-element.180), channel_id=1, source_target_pairs={{0,1},{1,2},{2,3},{3,4},{4,5},{5,6},{6,7},{8,9},{9,10},{10,11},{11... | collective-permute-start | bytes 4760 | tf_op jit(solution)/shard_map/while/body/eval_jaxpr/ppermute | solution.py:16
  872.8 24.8 %all-to-all-start = ((f32[64,1,192]{2,1,0:T(1,128)}), f32[64,1,192]{2,1,0:T(1,128)S(1)}, u32[]{:S(2)}, u32[]{:S(2)}) async-start(f32[64,1,192]{2,1,0:T(1,128)} %reshape.136), calls=%async_computation | async-start | bytes 131072 | tf_op jit(solution)/shard_map/while/body/eval_jaxpr/all_to_all | solution.py:42
  891.0 29.1 %collective-permute-start.2 = (f32[6,66,1]{2,1,0:T(8,128)S(1)}, f32[6,66,1]{2,1,0:T(8,128)S(1)}, u32[]{:S(2)}, u32[]{:S(2)}) collective-permute-start(f32[6,66,1]{2,1,0:T(8,128)S(1)} %get-tuple-element.180), channel_id=1, source_target_pairs={{0,1},{1,2},{2,3},{3,4},{4,5},{5,6},{6,7},{8,9},{9,10},{10,11},{11... | collective-permute-start | bytes 4760 | tf_op jit(solution)/shard_map/while/body/eval_jaxpr/ppermute | solution.py:16
  935.5 24.8 %all-to-all-start = ((f32[64,1,192]{2,1,0:T(1,128)}), f32[64,1,192]{2,1,0:T(1,128)S(1)}, u32[]{:S(2)}, u32[]{:S(2)}) async-start(f32[64,1,192]{2,1,0:T(1,128)} %reshape.136), calls=%async_computation | async-start | bytes 131072 | tf_op jit(solution)/shard_map/while/body/eval_jaxpr/all_to_all | solution.py:42
  953.8 29.1 %collective-permute-start.2 = (f32[6,66,1]{2,1,0:T(8,128)S(1)}, f32[6,66,1]{2,1,0:T(8,128)S(1)}, u32[]{:S(2)}, u32[]{:S(2)}) collective-permute-start(f32[6,66,1]{2,1,0:T(8,128)S(1)} %get-tuple-element.180), channel_id=1, source_target_pairs={{0,1},{1,2},{2,3},{3,4},{4,5},{5,6},{6,7},{8,9},{9,10},{10,11},{11... | collective-permute-start | bytes 4760 | tf_op jit(solution)/shard_map/while/body/eval_jaxpr/ppermute | solution.py:16
  998.2 24.8 %all-to-all-start = ((f32[64,1,192]{2,1,0:T(1,128)}), f32[64,1,192]{2,1,0:T(1,128)S(1)}, u32[]{:S(2)}, u32[]{:S(2)}) async-start(f32[64,1,192]{2,1,0:T(1,128)} %reshape.136), calls=%async_computation | async-start | bytes 131072 | tf_op jit(solution)/shard_map/while/body/eval_jaxpr/all_to_all | solution.py:42
  1016.5 29.1 %collective-permute-start.2 = (f32[6,66,1]{2,1,0:T(8,128)S(1)}, f32[6,66,1]{2,1,0:T(8,128)S(1)}, u32[]{:S(2)}, u32[]{:S(2)}) collective-permute-start(f32[6,66,1]{2,1,0:T(8,128)S(1)} %get-tuple-element.180), channel_id=1, source_target_pairs={{0,1},{1,2},{2,3},{3,4},{4,5},{5,6},{6,7},{8,9},{9,10},{10,11},{11... | collective-permute-start | bytes 4760 | tf_op jit(solution)/shard_map/while/body/eval_jaxpr/ppermute | solution.py:16
  1061.0 24.8 %all-to-all-start = ((f32[64,1,192]{2,1,0:T(1,128)}), f32[64,1,192]{2,1,0:T(1,128)S(1)}, u32[]{:S(2)}, u32[]{:S(2)}) async-start(f32[64,1,192]{2,1,0:T(1,128)} %reshape.136), calls=%async_computation | async-start | bytes 131072 | tf_op jit(solution)/shard_map/while/body/eval_jaxpr/all_to_all | solution.py:42
  1079.2 29.1 %collective-permute-start.2 = (f32[6,66,1]{2,1,0:T(8,128)S(1)}, f32[6,66,1]{2,1,0:T(8,128)S(1)}, u32[]{:S(2)}, u32[]{:S(2)}) collective-permute-start(f32[6,66,1]{2,1,0:T(8,128)S(1)} %get-tuple-element.180), channel_id=1, source_target_pairs={{0,1},{1,2},{2,3},{3,4},{4,5},{5,6},{6,7},{8,9},{9,10},{10,11},{11... | collective-permute-start | bytes 4760 | tf_op jit(solution)/shard_map/while/body/eval_jaxpr/ppermute | solution.py:16
  1123.7 24.8 %all-to-all-start = ((f32[64,1,192]{2,1,0:T(1,128)}), f32[64,1,192]{2,1,0:T(1,128)S(1)}, u32[]{:S(2)}, u32[]{:S(2)}) async-start(f32[64,1,192]{2,1,0:T(1,128)} %reshape.136), calls=%async_computation | async-start | bytes 131072 | tf_op jit(solution)/shard_map/while/body/eval_jaxpr/all_to_all | solution.py:42
  1142.0 29.1 %collective-permute-start.2 = (f32[6,66,1]{2,1,0:T(8,128)S(1)}, f32[6,66,1]{2,1,0:T(8,128)S(1)}, u32[]{:S(2)}, u32[]{:S(2)}) collective-permute-start(f32[6,66,1]{2,1,0:T(8,128)S(1)} %get-tuple-element.180), channel_id=1, source_target_pairs={{0,1},{1,2},{2,3},{3,4},{4,5},{5,6},{6,7},{8,9},{9,10},{10,11},{11... | collective-permute-start | bytes 4760 | tf_op jit(solution)/shard_map/while/body/eval_jaxpr/ppermute | solution.py:16
  1186.5 24.8 %all-to-all-start = ((f32[64,1,192]{2,1,0:T(1,128)}), f32[64,1,192]{2,1,0:T(1,128)S(1)}, u32[]{:S(2)}, u32[]{:S(2)}) async-start(f32[64,1,192]{2,1,0:T(1,128)} %reshape.136), calls=%async_computation | async-start | bytes 131072 | tf_op jit(solution)/shard_map/while/body/eval_jaxpr/all_to_all | solution.py:42
  1204.7 29.1 %collective-permute-start.2 = (f32[6,66,1]{2,1,0:T(8,128)S(1)}, f32[6,66,1]{2,1,0:T(8,128)S(1)}, u32[]{:S(2)}, u32[]{:S(2)}) collective-permute-start(f32[6,66,1]{2,1,0:T(8,128)S(1)} %get-tuple-element.180), channel_id=1, source_target_pairs={{0,1},{1,2},{2,3},{3,4},{4,5},{5,6},{6,7},{8,9},{9,10},{10,11},{11... | collective-permute-start | bytes 4760 | tf_op jit(solution)/shard_map/while/body/eval_jaxpr/ppermute | solution.py:16
  1249.2 24.8 %all-to-all-start = ((f32[64,1,192]{2,1,0:T(1,128)}), f32[64,1,192]{2,1,0:T(1,128)S(1)}, u32[]{:S(2)}, u32[]{:S(2)}) async-start(f32[64,1,192]{2,1,0:T(1,128)} %reshape.136), calls=%async_computation | async-start | bytes 131072 | tf_op jit(solution)/shard_map/while/body/eval_jaxpr/all_to_all | solution.py:42
  1267.5 29.1 %collective-permute-start.2 = (f32[6,66,1]{2,1,0:T(8,128)S(1)}, f32[6,66,1]{2,1,0:T(8,128)S(1)}, u32[]{:S(2)}, u32[]{:S(2)}) collective-permute-start(f32[6,66,1]{2,1,0:T(8,128)S(1)} %get-tuple-element.180), channel_id=1, source_target_pairs={{0,1},{1,2},{2,3},{3,4},{4,5},{5,6},{6,7},{8,9},{9,10},{10,11},{11... | collective-permute-start | bytes 4760 | tf_op jit(solution)/shard_map/while/body/eval_jaxpr/ppermute | solution.py:16
  (144 other events, 3909.9 us)
Sparse Core Ops, SparseCore 0:
  1299.2 48.4 all-reduce.1
where the time goes:
time: 1380 us; the launch traced here: 1370 us
  starting transfers between devices  458 us (33%)
  local copies, waits for them, and re-layouts  429 us (31%)
  other arithmetic  355 us (26%)
  waiting for transfers between devices  113 us (8%)
  between operations  14.9 us (1%)
    scatter-add x20, other arithmetic, mortar(): added = jnp.zeros((6, cells), jnp.float32).at[:, targets].add(got * weights)  304 us
    all_to_all x20, starting transfers between devices, mortar(): lax.all_to_all(sent, ('mx', 'my'), split_axis=1, concat_axis=1, tiled=True)  219 us
    gather x20, local copies, waits for them, and re-layouts, mortar(): sent = field.reshape(6, cells)[:, sources]  177 us
    ppermute x44, starting transfers between devices, extended(): before = lax.ppermute(last, axis, up)  149 us
    reshape x20, local copies, waits for them, and re-layouts, mortar(): return added.reshape(6, rows_x, rows_y)  106 us
    another operation x20, local copies, waits for them, and re-layouts  94.6 us
    ppermute x44, starting transfers between devices, extended(): after = lax.ppermute(first, axis, down)  89.9 us
    ppermute x44, waiting for transfers between devices, extended(): before = lax.ppermute(last, axis, up)  59.5 us
  transfers between devices with their start and end apart: 109, of which 25 were waited for; matrix products, arithmetic and copies ran while one was open for 34% of the time, Pallas kernels for 0%

commit v1 on v0

--- a/solution.py
+++ b/solution.py
@@ -68,7 +68,9 @@
     t_re = da * u[:3] - db * u[3:] - dstiff * nb[:3]
     t_im = da * u[3:] + db * u[:3] - dstiff * nb[3:]
     sens = -jnp.sum(field[:3] * t_re - field[3:] * t_im, axis=0)
-    total = lax.psum(sens, "freq")
+    total = sens
+    for hop in (1, 2):
+        total = total + lax.ppermute(total, "freq", [(dev, dev ^ hop) for dev in range(4)])
     weighted = extended(density * total, (("mx", 0), ("my", 1)), 1)
     filt = weighted[1:-1, 1:-1]
     filt = filt + 0.5 * (

time: 1380 us -> 1330 us (0.964)
  waiting for transfers between devices: 113 us -> 70.1 us
    psum x1 -> x0, waiting for transfers between devices: 48.6 us -> none  [on_device(): total = lax.psum(sens, 'freq')]
  transfers between devices with their start and end apart: 109 -> 110, of which waited for: 25 -> 26; matrix products, arithmetic and copies ran while one was open for 34% -> 35% of each run, Pallas kernels for 0% -> 0%
where the time goes in v1:
time: 1330 us; the launch traced here: 1320 us
  starting transfers between devices  463 us (35%)
  local copies, waits for them, and re-layouts  429 us (32%)
  other arithmetic  355 us (27%)
  waiting for transfers between devices  70.1 us (5%)
    scatter-add x20, other arithmetic, mortar(): added = jnp.zeros((6, cells), jnp.float32).at[:, targets].add(got * weights)  304 us
    all_to_all x20, starting transfers between devices, mortar(): lax.all_to_all(sent, ('mx', 'my'), split_axis=1, concat_axis=1, tiled=True)  219 us
    gather x20, local copies, waits for them, and re-layouts, mortar(): sent = field.reshape(6, cells)[:, sources]  177 us
    ppermute x44, starting transfers between devices, extended(): before = lax.ppermute(last, axis, up)  149 us
    reshape x20, local copies, waits for them, and re-layouts, mortar(): return added.reshape(6, rows_x, rows_y)  106 us
    another operation x20, local copies, waits for them, and re-layouts  94.6 us
    ppermute x44, starting transfers between devices, extended(): after = lax.ppermute(first, axis, down)  89.9 us
    ppermute x44, waiting for transfers between devices, extended(): before = lax.ppermute(last, axis, up)  59.5 us
  transfers between devices with their start and end apart: 110, of which 26 were waited for; matrix products, arithmetic and copies ran while one was open for 35% of the time, Pallas kernels for 0%

profile of v1, /device:TPU:98, one launch (start us, length us, event | category | flops | bytes accessed | tf_op | source)
XLA Modules:
  0.0 1323.7 jit_solution(1392814870038724644)
XLA Ops:
  7.1 11.6 scatter_custom_fusion.1
  35.1 1255.2 %while.10 = (s32[]{:T(128)}, f32[6,64,256]{2,1,0:T(8,128)S(1)}, f32[64,256]{1,0:T(8,128)S(1)}, f32[6,64,256]{2,1,0:T(8,128)}, s32[2048]{0:T(1024)}, /*index=5*/s...) while((s32[]{:T(128)}, f32[6,64,256]{2,1,0:T(8,128)S(1)}, ...), condition=%wide.region_3.0_spmd, body=%wide.region_1.0_spmd.sunk | while | flops 2109442 | bytes 9095261 | solution.py:56
  50.1 11.4 all-to-all-start
  77.3 15.2 %scatter_custom_fusion.7 = f32[6,16384]{0,1:T(8,128)} fusion(s32[2048]{0:T(1024)S(1)} %bitcast.65, f32[2048,6]{1,0:T(8,128)S(1)} %copy.34, f32[]{:T(128)} %constant.21.clone.1..sunk), kind=kCustom, calls=%fused_computation.3.clone.1 | custom fusion | flops 12288 | bytes 393220 | tf_op jit(solution)/shard_map/while/body/eval_jaxpr/scatter-add | solution.py:43
  103.2 8.8 gather_fusion
  113.3 10.9 all-to-all-start
  140.0 15.2 %scatter_custom_fusion.7 = f32[6,16384]{0,1:T(8,128)} fusion(s32[2048]{0:T(1024)S(1)} %bitcast.65, f32[2048,6]{1,0:T(8,128)S(1)} %copy.34, f32[]{:T(128)} %constant.21.clone.1..sunk), kind=kCustom, calls=%fused_computation.3.clone.1 | custom fusion | flops 12288 | bytes 393220 | tf_op jit(solution)/shard_map/while/body/eval_jaxpr/scatter-add | solution.py:43
  176.0 10.9 all-to-all-start
  202.8 15.2 %scatter_custom_fusion.7 = f32[6,16384]{0,1:T(8,128)} fusion(s32[2048]{0:T(1024)S(1)} %bitcast.65, f32[2048,6]{1,0:T(8,128)S(1)} %copy.34, f32[]{:T(128)} %constant.21.clone.1..sunk), kind=kCustom, calls=%fused_computation.3.clone.1 | custom fusion | flops 12288 | bytes 393220 | tf_op jit(solution)/shard_map/while/body/eval_jaxpr/scatter-add | solution.py:43
  238.7 10.9 all-to-all-start
  265.5 15.2 %scatter_custom_fusion.7 = f32[6,16384]{0,1:T(8,128)} fusion(s32[2048]{0:T(1024)S(1)} %bitcast.65, f32[2048,6]{1,0:T(8,128)S(1)} %copy.34, f32[]{:T(128)} %constant.21.clone.1..sunk), kind=kCustom, calls=%fused_computation.3.clone.1 | custom fusion | flops 12288 | bytes 393220 | tf_op jit(solution)/shard_map/while/body/eval_jaxpr/scatter-add | solution.py:43
  291.4 8.8 gather_fusion
  301.5 10.9 all-to-all-start
  328.3 15.2 %scatter_custom_fusion.7 = f32[6,16384]{0,1:T(8,128)} fusion(s32[2048]{0:T(1024)S(1)} %bitcast.65, f32[2048,6]{1,0:T(8,128)S(1)} %copy.34, f32[]{:T(128)} %constant.21.clone.1..sunk), kind=kCustom, calls=%fused_computation.3.clone.1 | custom fusion | flops 12288 | bytes 393220 | tf_op jit(solution)/shard_map/while/body/eval_jaxpr/scatter-add | solution.py:43
  364.2 10.9 all-to-all-start
  391.0 15.2 %scatter_custom_fusion.7 = f32[6,16384]{0,1:T(8,128)} fusion(s32[2048]{0:T(1024)S(1)} %bitcast.65, f32[2048,6]{1,0:T(8,128)S(1)} %copy.34, f32[]{:T(128)} %constant.21.clone.1..sunk), kind=kCustom, calls=%fused_computation.3.clone.1 | custom fusion | flops 12288 | bytes 393220 | tf_op jit(solution)/shard_map/while/body/eval_jaxpr/scatter-add | solution.py:43
  427.0 10.9 all-to-all-start
  453.7 15.2 %scatter_custom_fusion.7 = f32[6,16384]{0,1:T(8,128)} fusion(s32[2048]{0:T(1024)S(1)} %bitcast.65, f32[2048,6]{1,0:T(8,128)S(1)} %copy.34, f32[]{:T(128)} %constant.21.clone.1..sunk), kind=kCustom, calls=%fused_computation.3.clone.1 | custom fusion | flops 12288 | bytes 393220 | tf_op jit(solution)/shard_map/while/body/eval_jaxpr/scatter-add | solution.py:43
  479.6 8.8 gather_fusion
  489.7 10.9 all-to-all-start
  516.5 15.2 %scatter_custom_fusion.7 = f32[6,16384]{0,1:T(8,128)} fusion(s32[2048]{0:T(1024)S(1)} %bitcast.65, f32[2048,6]{1,0:T(8,128)S(1)} %copy.34, f32[]{:T(128)} %constant.21.clone.1..sunk), kind=kCustom, calls=%fused_computation.3.clone.1 | custom fusion | flops 12288 | bytes 393220 | tf_op jit(solution)/shard_map/while/body/eval_jaxpr/scatter-add | solution.py:43
  552.4 10.9 all-to-all-start
  579.2 15.2 %scatter_custom_fusion.7 = f32[6,16384]{0,1:T(8,128)} fusion(s32[2048]{0:T(1024)S(1)} %bitcast.65, f32[2048,6]{1,0:T(8,128)S(1)} %copy.34, f32[]{:T(128)} %constant.21.clone.1..sunk), kind=kCustom, calls=%fused_computation.3.clone.1 | custom fusion | flops 12288 | bytes 393220 | tf_op jit(solution)/shard_map/while/body/eval_jaxpr/scatter-add | solution.py:43
  605.1 8.8 gather_fusion
  615.2 10.9 all-to-all-start
  642.0 15.2 %scatter_custom_fusion.7 = f32[6,16384]{0,1:T(8,128)} fusion(s32[2048]{0:T(1024)S(1)} %bitcast.65, f32[2048,6]{1,0:T(8,128)S(1)} %copy.34, f32[]{:T(128)} %constant.21.clone.1..sunk), kind=kCustom, calls=%fused_computation.3.clone.1 | custom fusion | flops 12288 | bytes 393220 | tf_op jit(solution)/shard_map/while/body/eval_jaxpr/scatter-add | solution.py:43
  677.9 10.9 all-to-all-start
  704.7 15.2 %scatter_custom_fusion.7 = f32[6,16384]{0,1:T(8,128)} fusion(s32[2048]{0:T(1024)S(1)} %bitcast.65, f32[2048,6]{1,0:T(8,128)S(1)} %copy.34, f32[]{:T(128)} %constant.21.clone.1..sunk), kind=kCustom, calls=%fused_computation.3.clone.1 | custom fusion | flops 12288 | bytes 393220 | tf_op jit(solution)/shard_map/while/body/eval_jaxpr/scatter-add | solution.py:43
  740.6 10.9 all-to-all-start
  767.4 15.2 %scatter_custom_fusion.7 = f32[6,16384]{0,1:T(8,128)} fusion(s32[2048]{0:T(1024)S(1)} %bitcast.65, f32[2048,6]{1,0:T(8,128)S(1)} %copy.34, f32[]{:T(128)} %constant.21.clone.1..sunk), kind=kCustom, calls=%fused_computation.3.clone.1 | custom fusion | flops 12288 | bytes 393220 | tf_op jit(solution)/shard_map/while/body/eval_jaxpr/scatter-add | solution.py:43
  793.3 8.8 gather_fusion
  803.4 10.9 all-to-all-start
  830.2 15.2 %scatter_custom_fusion.7 = f32[6,16384]{0,1:T(8,128)} fusion(s32[2048]{0:T(1024)S(1)} %bitcast.65, f32[2048,6]{1,0:T(8,128)S(1)} %copy.34, f32[]{:T(128)} %constant.21.clone.1..sunk), kind=kCustom, calls=%fused_computation.3.clone.1 | custom fusion | flops 12288 | bytes 393220 | tf_op jit(solution)/shard_map/while/body/eval_jaxpr/scatter-add | solution.py:43
  866.1 10.9 all-to-all-start
  892.9 15.2 %scatter_custom_fusion.7 = f32[6,16384]{0,1:T(8,128)} fusion(s32[2048]{0:T(1024)S(1)} %bitcast.65, f32[2048,6]{1,0:T(8,128)S(1)} %copy.34, f32[]{:T(128)} %constant.21.clone.1..sunk), kind=kCustom, calls=%fused_computation.3.clone.1 | custom fusion | flops 12288 | bytes 393220 | tf_op jit(solution)/shard_map/while/body/eval_jaxpr/scatter-add | solution.py:43
  928.9 10.9 all-to-all-start
  955.7 15.2 %scatter_custom_fusion.7 = f32[6,16384]{0,1:T(8,128)} fusion(s32[2048]{0:T(1024)S(1)} %bitcast.65, f32[2048,6]{1,0:T(8,128)S(1)} %copy.34, f32[]{:T(128)} %constant.21.clone.1..sunk), kind=kCustom, calls=%fused_computation.3.clone.1 | custom fusion | flops 12288 | bytes 393220 | tf_op jit(solution)/shard_map/while/body/eval_jaxpr/scatter-add | solution.py:43
  981.5 8.8 gather_fusion
  991.6 10.9 all-to-all-start
  1018.4 15.2 %scatter_custom_fusion.7 = f32[6,16384]{0,1:T(8,128)} fusion(s32[2048]{0:T(1024)S(1)} %bitcast.65, f32[2048,6]{1,0:T(8,128)S(1)} %copy.34, f32[]{:T(128)} %constant.21.clone.1..sunk), kind=kCustom, calls=%fused_computation.3.clone.1 | custom fusion | flops 12288 | bytes 393220 | tf_op jit(solution)/shard_map/while/body/eval_jaxpr/scatter-add | solution.py:43
  1054.3 10.9 all-to-all-start
  1081.1 15.2 %scatter_custom_fusion.7 = f32[6,16384]{0,1:T(8,128)} fusion(s32[2048]{0:T(1024)S(1)} %bitcast.65, f32[2048,6]{1,0:T(8,128)S(1)} %copy.34, f32[]{:T(128)} %constant.21.clone.1..sunk), kind=kCustom, calls=%fused_computation.3.clone.1 | custom fusion | flops 12288 | bytes 393220 | tf_op jit(solution)/shard_map/while/body/eval_jaxpr/scatter-add | solution.py:43
  1117.1 10.9 all-to-all-start
  1143.9 15.2 %scatter_custom_fusion.7 = f32[6,16384]{0,1:T(8,128)} fusion(s32[2048]{0:T(1024)S(1)} %bitcast.65, f32[2048,6]{1,0:T(8,128)S(1)} %copy.34, f32[]{:T(128)} %constant.21.clone.1..sunk), kind=kCustom, calls=%fused_computation.3.clone.1 | custom fusion | flops 12288 | bytes 393220 | tf_op jit(solution)/shard_map/while/body/eval_jaxpr/scatter-add | solution.py:43
  1179.8 10.9 all-to-all-start
  1206.6 15.2 %scatter_custom_fusion.7 = f32[6,16384]{0,1:T(8,128)} fusion(s32[2048]{0:T(1024)S(1)} %bitcast.65, f32[2048,6]{1,0:T(8,128)S(1)} %copy.34, f32[]{:T(128)} %constant.21.clone.1..sunk), kind=kCustom, calls=%fused_computation.3.clone.1 | custom fusion | flops 12288 | bytes 393220 | tf_op jit(solution)/shard_map/while/body/eval_jaxpr/scatter-add | solution.py:43
  1242.6 10.9 all-to-all-start
  1269.3 15.2 %scatter_custom_fusion.7 = f32[6,16384]{0,1:T(8,128)} fusion(s32[2048]{0:T(1024)S(1)} %bitcast.65, f32[2048,6]{1,0:T(8,128)S(1)} %copy.34, f32[]{:T(128)} %constant.21.clone.1..sunk), kind=kCustom, calls=%fused_computation.3.clone.1 | custom fusion | flops 12288 | bytes 393220 | tf_op jit(solution)/shard_map/while/body/eval_jaxpr/scatter-add | solution.py:43
  (796 shorter events, 729.4 us)
Async XLA Ops:
  50.1 25.2 %all-to-all-start = ((f32[64,1,192]{2,1,0:T(1,128)}), f32[64,1,192]{2,1,0:T(1,128)S(1)}, u32[]{:S(2)}, u32[]{:S(2)}) async-start(f32[64,1,192]{2,1,0:T(1,128)} %reshape.136), calls=%async_computation | async-start | bytes 131072 | tf_op jit(solution)/shard_map/while/body/eval_jaxpr/all_to_all | solution.py:42
  68.8 29.1 %collective-permute-start.2 = (f32[6,66,1]{2,1,0:T(8,128)S(1)}, f32[6,66,1]{2,1,0:T(8,128)S(1)}, u32[]{:S(2)}, u32[]{:S(2)}) collective-permute-start(f32[6,66,1]{2,1,0:T(8,128)S(1)} %get-tuple-element.180), channel_id=1, source_target_pairs={{0,1},{1,2},{2,3},{3,4},{4,5},{5,6},{6,7},{8,9},{9,10},{10,11},{11... | collective-permute-start | bytes 4760 | tf_op jit(solution)/shard_map/while/body/eval_jaxpr/ppermute | solution.py:16
  73.4 24.5 %collective-permute-start.3 = (f32[6,66,1]{2,1,0:T(8,128)S(1)}, f32[6,66,1]{2,1,0:T(8,128)S(1)}, u32[]{:S(2)}, u32[]{:S(2)}) collective-permute-start(f32[6,66,1]{2,1,0:T(8,128)S(1)} %get-tuple-element.181), channel_id=1, source_target_pairs={{1,0},{2,1},{3,2},{4,3},{5,4},{6,5},{7,6},{9,8},{10,9},{11,10},{12... | collective-permute-start | bytes 4760 | tf_op jit(solution)/shard_map/while/body/eval_jaxpr/ppermute | solution.py:17
  113.3 24.8 %all-to-all-start = ((f32[64,1,192]{2,1,0:T(1,128)}), f32[64,1,192]{2,1,0:T(1,128)S(1)}, u32[]{:S(2)}, u32[]{:S(2)}) async-start(f32[64,1,192]{2,1,0:T(1,128)} %reshape.136), calls=%async_computation | async-start | bytes 131072 | tf_op jit(solution)/shard_map/while/body/eval_jaxpr/all_to_all | solution.py:42
  131.5 29.1 %collective-permute-start.2 = (f32[6,66,1]{2,1,0:T(8,128)S(1)}, f32[6,66,1]{2,1,0:T(8,128)S(1)}, u32[]{:S(2)}, u32[]{:S(2)}) collective-permute-start(f32[6,66,1]{2,1,0:T(8,128)S(1)} %get-tuple-element.180), channel_id=1, source_target_pairs={{0,1},{1,2},{2,3},{3,4},{4,5},{5,6},{6,7},{8,9},{9,10},{10,11},{11... | collective-permute-start | bytes 4760 | tf_op jit(solution)/shard_map/while/body/eval_jaxpr/ppermute | solution.py:16
  176.0 24.8 %all-to-all-start = ((f32[64,1,192]{2,1,0:T(1,128)}), f32[64,1,192]{2,1,0:T(1,128)S(1)}, u32[]{:S(2)}, u32[]{:S(2)}) async-start(f32[64,1,192]{2,1,0:T(1,128)} %reshape.136), calls=%async_computation | async-start | bytes 131072 | tf_op jit(solution)/shard_map/while/body/eval_jaxpr/all_to_all | solution.py:42
  194.2 29.1 %collective-permute-start.2 = (f32[6,66,1]{2,1,0:T(8,128)S(1)}, f32[6,66,1]{2,1,0:T(8,128)S(1)}, u32[]{:S(2)}, u32[]{:S(2)}) collective-permute-start(f32[6,66,1]{2,1,0:T(8,128)S(1)} %get-tuple-element.180), channel_id=1, source_target_pairs={{0,1},{1,2},{2,3},{3,4},{4,5},{5,6},{6,7},{8,9},{9,10},{10,11},{11... | collective-permute-start | bytes 4760 | tf_op jit(solution)/shard_map/while/body/eval_jaxpr/ppermute | solution.py:16
  198.8 24.5 %collective-permute-start.3 = (f32[6,66,1]{2,1,0:T(8,128)S(1)}, f32[6,66,1]{2,1,0:T(8,128)S(1)}, u32[]{:S(2)}, u32[]{:S(2)}) collective-permute-start(f32[6,66,1]{2,1,0:T(8,128)S(1)} %get-tuple-element.181), channel_id=1, source_target_pairs={{1,0},{2,1},{3,2},{4,3},{5,4},{6,5},{7,6},{9,8},{10,9},{11,10},{12... | collective-permute-start | bytes 4760 | tf_op jit(solution)/shard_map/while/body/eval_jaxpr/ppermute | solution.py:17
  238.7 24.8 %all-to-all-start = ((f32[64,1,192]{2,1,0:T(1,128)}), f32[64,1,192]{2,1,0:T(1,128)S(1)}, u32[]{:S(2)}, u32[]{:S(2)}) async-start(f32[64,1,192]{2,1,0:T(1,128)} %reshape.136), calls=%async_computation | async-start | bytes 131072 | tf_op jit(solution)/shard_map/while/body/eval_jaxpr/all_to_all | solution.py:42
  257.0 29.1 %collective-permute-start.2 = (f32[6,66,1]{2,1,0:T(8,128)S(1)}, f32[6,66,1]{2,1,0:T(8,128)S(1)}, u32[]{:S(2)}, u32[]{:S(2)}) collective-permute-start(f32[6,66,1]{2,1,0:T(8,128)S(1)} %get-tuple-element.180), channel_id=1, source_target_pairs={{0,1},{1,2},{2,3},{3,4},{4,5},{5,6},{6,7},{8,9},{9,10},{10,11},{11... | collective-permute-start | bytes 4760 | tf_op jit(solution)/shard_map/while/body/eval_jaxpr/ppermute | solution.py:16
  261.6 24.5 %collective-permute-start.3 = (f32[6,66,1]{2,1,0:T(8,128)S(1)}, f32[6,66,1]{2,1,0:T(8,128)S(1)}, u32[]{:S(2)}, u32[]{:S(2)}) collective-permute-start(f32[6,66,1]{2,1,0:T(8,128)S(1)} %get-tuple-element.181), channel_id=1, source_target_pairs={{1,0},{2,1},{3,2},{4,3},{5,4},{6,5},{7,6},{9,8},{10,9},{11,10},{12... | collective-permute-start | bytes 4760 | tf_op jit(solution)/shard_map/while/body/eval_jaxpr/ppermute | solution.py:17
  301.5 24.8 %all-to-all-start = ((f32[64,1,192]{2,1,0:T(1,128)}), f32[64,1,192]{2,1,0:T(1,128)S(1)}, u32[]{:S(2)}, u32[]{:S(2)}) async-start(f32[64,1,192]{2,1,0:T(1,128)} %reshape.136), calls=%async_computation | async-start | bytes 131072 | tf_op jit(solution)/shard_map/while/body/eval_jaxpr/all_to_all | solution.py:42
  319.7 29.1 %collective-permute-start.2 = (f32[6,66,1]{2,1,0:T(8,128)S(1)}, f32[6,66,1]{2,1,0:T(8,128)S(1)}, u32[]{:S(2)}, u32[]{:S(2)}) collective-permute-start(f32[6,66,1]{2,1,0:T(8,128)S(1)} %get-tuple-element.180), channel_id=1, source_target_pairs={{0,1},{1,2},{2,3},{3,4},{4,5},{5,6},{6,7},{8,9},{9,10},{10,11},{11... | collective-permute-start | bytes 4760 | tf_op jit(solution)/shard_map/while/body/eval_jaxpr/ppermute | solution.py:16
  364.2 24.8 %all-to-all-start = ((f32[64,1,192]{2,1,0:T(1,128)}), f32[64,1,192]{2,1,0:T(1,128)S(1)}, u32[]{:S(2)}, u32[]{:S(2)}) async-start(f32[64,1,192]{2,1,0:T(1,128)} %reshape.136), calls=%async_computation | async-start | bytes 131072 | tf_op jit(solution)/shard_map/while/body/eval_jaxpr/all_to_all | solution.py:42
  382.5 29.1 %collective-permute-start.2 = (f32[6,66,1]{2,1,0:T(8,128)S(1)}, f32[6,66,1]{2,1,0:T(8,128)S(1)}, u32[]{:S(2)}, u32[]{:S(2)}) collective-permute-start(f32[6,66,1]{2,1,0:T(8,128)S(1)} %get-tuple-element.180), channel_id=1, source_target_pairs={{0,1},{1,2},{2,3},{3,4},{4,5},{5,6},{6,7},{8,9},{9,10},{10,11},{11... | collective-permute-start | bytes 4760 | tf_op jit(solution)/shard_map/while/body/eval_jaxpr/ppermute | solution.py:16
  387.1 24.5 %collective-permute-start.3 = (f32[6,66,1]{2,1,0:T(8,128)S(1)}, f32[6,66,1]{2,1,0:T(8,128)S(1)}, u32[]{:S(2)}, u32[]{:S(2)}) collective-permute-start(f32[6,66,1]{2,1,0:T(8,128)S(1)} %get-tuple-element.181), channel_id=1, source_target_pairs={{1,0},{2,1},{3,2},{4,3},{5,4},{6,5},{7,6},{9,8},{10,9},{11,10},{12... | collective-permute-start | bytes 4760 | tf_op jit(solution)/shard_map/while/body/eval_jaxpr/ppermute | solution.py:17
  427.0 24.8 %all-to-all-start = ((f32[64,1,192]{2,1,0:T(1,128)}), f32[64,1,192]{2,1,0:T(1,128)S(1)}, u32[]{:S(2)}, u32[]{:S(2)}) async-start(f32[64,1,192]{2,1,0:T(1,128)} %reshape.136), calls=%async_computation | async-start | bytes 131072 | tf_op jit(solution)/shard_map/while/body/eval_jaxpr/all_to_all | solution.py:42
  445.2 29.1 %collective-permute-start.2 = (f32[6,66,1]{2,1,0:T(8,128)S(1)}, f32[6,66,1]{2,1,0:T(8,128)S(1)}, u32[]{:S(2)}, u32[]{:S(2)}) collective-permute-start(f32[6,66,1]{2,1,0:T(8,128)S(1)} %get-tuple-element.180), channel_id=1, source_target_pairs={{0,1},{1,2},{2,3},{3,4},{4,5},{5,6},{6,7},{8,9},{9,10},{10,11},{11... | collective-permute-start | bytes 4760 | tf_op jit(solution)/shard_map/while/body/eval_jaxpr/ppermute | solution.py:16
  449.8 24.5 %collective-permute-start.3 = (f32[6,66,1]{2,1,0:T(8,128)S(1)}, f32[6,66,1]{2,1,0:T(8,128)S(1)}, u32[]{:S(2)}, u32[]{:S(2)}) collective-permute-start(f32[6,66,1]{2,1,0:T(8,128)S(1)} %get-tuple-element.181), channel_id=1, source_target_pairs={{1,0},{2,1},{3,2},{4,3},{5,4},{6,5},{7,6},{9,8},{10,9},{11,10},{12... | collective-permute-start | bytes 4760 | tf_op jit(solution)/shard_map/while/body/eval_jaxpr/ppermute | solution.py:17
  489.7 24.8 %all-to-all-start = ((f32[64,1,192]{2,1,0:T(1,128)}), f32[64,1,192]{2,1,0:T(1,128)S(1)}, u32[]{:S(2)}, u32[]{:S(2)}) async-start(f32[64,1,192]{2,1,0:T(1,128)} %reshape.136), calls=%async_computation | async-start | bytes 131072 | tf_op jit(solution)/shard_map/while/body/eval_jaxpr/all_to_all | solution.py:42
  507.9 29.1 %collective-permute-start.2 = (f32[6,66,1]{2,1,0:T(8,128)S(1)}, f32[6,66,1]{2,1,0:T(8,128)S(1)}, u32[]{:S(2)}, u32[]{:S(2)}) collective-permute-start(f32[6,66,1]{2,1,0:T(8,128)S(1)} %get-tuple-element.180), channel_id=1, source_target_pairs={{0,1},{1,2},{2,3},{3,4},{4,5},{5,6},{6,7},{8,9},{9,10},{10,11},{11... | collective-permute-start | bytes 4760 | tf_op jit(solution)/shard_map/while/body/eval_jaxpr/ppermute | solution.py:16
  552.4 24.8 %all-to-all-start = ((f32[64,1,192]{2,1,0:T(1,128)}), f32[64,1,192]{2,1,0:T(1,128)S(1)}, u32[]{:S(2)}, u32[]{:S(2)}) async-start(f32[64,1,192]{2,1,0:T(1,128)} %reshape.136), calls=%async_computation | async-start | bytes 131072 | tf_op jit(solution)/shard_map/while/body/eval_jaxpr/all_to_all | solution.py:42
  570.7 29.1 %collective-permute-start.2 = (f32[6,66,1]{2,1,0:T(8,128)S(1)}, f32[6,66,1]{2,1,0:T(8,128)S(1)}, u32[]{:S(2)}, u32[]{:S(2)}) collective-permute-start(f32[6,66,1]{2,1,0:T(8,128)S(1)} %get-tuple-element.180), channel_id=1, source_target_pairs={{0,1},{1,2},{2,3},{3,4},{4,5},{5,6},{6,7},{8,9},{9,10},{10,11},{11... | collective-permute-start | bytes 4760 | tf_op jit(solution)/shard_map/while/body/eval_jaxpr/ppermute | solution.py:16
  575.3 24.5 %collective-permute-start.3 = (f32[6,66,1]{2,1,0:T(8,128)S(1)}, f32[6,66,1]{2,1,0:T(8,128)S(1)}, u32[]{:S(2)}, u32[]{:S(2)}) collective-permute-start(f32[6,66,1]{2,1,0:T(8,128)S(1)} %get-tuple-element.181), channel_id=1, source_target_pairs={{1,0},{2,1},{3,2},{4,3},{5,4},{6,5},{7,6},{9,8},{10,9},{11,10},{12... | collective-permute-start | bytes 4760 | tf_op jit(solution)/shard_map/while/body/eval_jaxpr/ppermute | solution.py:17
  615.2 24.8 %all-to-all-start = ((f32[64,1,192]{2,1,0:T(1,128)}), f32[64,1,192]{2,1,0:T(1,128)S(1)}, u32[]{:S(2)}, u32[]{:S(2)}) async-start(f32[64,1,192]{2,1,0:T(1,128)} %reshape.136), calls=%async_computation | async-start | bytes 131072 | tf_op jit(solution)/shard_map/while/body/eval_jaxpr/all_to_all | solution.py:42
  633.4 29.1 %collective-permute-start.2 = (f32[6,66,1]{2,1,0:T(8,128)S(1)}, f32[6,66,1]{2,1,0:T(8,128)S(1)}, u32[]{:S(2)}, u32[]{:S(2)}) collective-permute-start(f32[6,66,1]{2,1,0:T(8,128)S(1)} %get-tuple-element.180), channel_id=1, source_target_pairs={{0,1},{1,2},{2,3},{3,4},{4,5},{5,6},{6,7},{8,9},{9,10},{10,11},{11... | collective-permute-start | bytes 4760 | tf_op jit(solution)/shard_map/while/body/eval_jaxpr/ppermute | solution.py:16
  638.0 24.5 %collective-permute-start.3 = (f32[6,66,1]{2,1,0:T(8,128)S(1)}, f32[6,66,1]{2,1,0:T(8,128)S(1)}, u32[]{:S(2)}, u32[]{:S(2)}) collective-permute-start(f32[6,66,1]{2,1,0:T(8,128)S(1)} %get-tuple-element.181), channel_id=1, source_target_pairs={{1,0},{2,1},{3,2},{4,3},{5,4},{6,5},{7,6},{9,8},{10,9},{11,10},{12... | collective-permute-start | bytes 4760 | tf_op jit(solution)/shard_map/while/body/eval_jaxpr/ppermute | solution.py:17
  677.9 24.8 %all-to-all-start = ((f32[64,1,192]{2,1,0:T(1,128)}), f32[64,1,192]{2,1,0:T(1,128)S(1)}, u32[]{:S(2)}, u32[]{:S(2)}) async-start(f32[64,1,192]{2,1,0:T(1,128)} %reshape.136), calls=%async_computation | async-start | bytes 131072 | tf_op jit(solution)/shard_map/while/body/eval_jaxpr/all_to_all | solution.py:42
  696.2 29.1 %collective-permute-start.2 = (f32[6,66,1]{2,1,0:T(8,128)S(1)}, f32[6,66,1]{2,1,0:T(8,128)S(1)}, u32[]{:S(2)}, u32[]{:S(2)}) collective-permute-start(f32[6,66,1]{2,1,0:T(8,128)S(1)} %get-tuple-element.180), channel_id=1, source_target_pairs={{0,1},{1,2},{2,3},{3,4},{4,5},{5,6},{6,7},{8,9},{9,10},{10,11},{11... | collective-permute-start | bytes 4760 | tf_op jit(solution)/shard_map/while/body/eval_jaxpr/ppermute | solution.py:16
  700.7 24.5 %collective-permute-start.3 = (f32[6,66,1]{2,1,0:T(8,128)S(1)}, f32[6,66,1]{2,1,0:T(8,128)S(1)}, u32[]{:S(2)}, u32[]{:S(2)}) collective-permute-start(f32[6,66,1]{2,1,0:T(8,128)S(1)} %get-tuple-element.181), channel_id=1, source_target_pairs={{1,0},{2,1},{3,2},{4,3},{5,4},{6,5},{7,6},{9,8},{10,9},{11,10},{12... | collective-permute-start | bytes 4760 | tf_op jit(solution)/shard_map/while/body/eval_jaxpr/ppermute | solution.py:17
  740.6 24.8 %all-to-all-start = ((f32[64,1,192]{2,1,0:T(1,128)}), f32[64,1,192]{2,1,0:T(1,128)S(1)}, u32[]{:S(2)}, u32[]{:S(2)}) async-start(f32[64,1,192]{2,1,0:T(1,128)} %reshape.136), calls=%async_computation | async-start | bytes 131072 | tf_op jit(solution)/shard_map/while/body/eval_jaxpr/all_to_all | solution.py:42
  758.9 29.1 %collective-permute-start.2 = (f32[6,66,1]{2,1,0:T(8,128)S(1)}, f32[6,66,1]{2,1,0:T(8,128)S(1)}, u32[]{:S(2)}, u32[]{:S(2)}) collective-permute-start(f32[6,66,1]{2,1,0:T(8,128)S(1)} %get-tuple-element.180), channel_id=1, source_target_pairs={{0,1},{1,2},{2,3},{3,4},{4,5},{5,6},{6,7},{8,9},{9,10},{10,11},{11... | collective-permute-start | bytes 4760 | tf_op jit(solution)/shard_map/while/body/eval_jaxpr/ppermute | solution.py:16
  803.4 24.8 %all-to-all-start = ((f32[64,1,192]{2,1,0:T(1,128)}), f32[64,1,192]{2,1,0:T(1,128)S(1)}, u32[]{:S(2)}, u32[]{:S(2)}) async-start(f32[64,1,192]{2,1,0:T(1,128)} %reshape.136), calls=%async_computation | async-start | bytes 131072 | tf_op jit(solution)/shard_map/while/body/eval_jaxpr/all_to_all | solution.py:42
  821.6 29.1 %collective-permute-start.2 = (f32[6,66,1]{2,1,0:T(8,128)S(1)}, f32[6,66,1]{2,1,0:T(8,128)S(1)}, u32[]{:S(2)}, u32[]{:S(2)}) collective-permute-start(f32[6,66,1]{2,1,0:T(8,128)S(1)} %get-tuple-element.180), channel_id=1, source_target_pairs={{0,1},{1,2},{2,3},{3,4},{4,5},{5,6},{6,7},{8,9},{9,10},{10,11},{11... | collective-permute-start | bytes 4760 | tf_op jit(solution)/shard_map/while/body/eval_jaxpr/ppermute | solution.py:16
  866.1 24.8 %all-to-all-start = ((f32[64,1,192]{2,1,0:T(1,128)}), f32[64,1,192]{2,1,0:T(1,128)S(1)}, u32[]{:S(2)}, u32[]{:S(2)}) async-start(f32[64,1,192]{2,1,0:T(1,128)} %reshape.136), calls=%async_computation | async-start | bytes 131072 | tf_op jit(solution)/shard_map/while/body/eval_jaxpr/all_to_all | solution.py:42
  884.4 29.1 %collective-permute-start.2 = (f32[6,66,1]{2,1,0:T(8,128)S(1)}, f32[6,66,1]{2,1,0:T(8,128)S(1)}, u32[]{:S(2)}, u32[]{:S(2)}) collective-permute-start(f32[6,66,1]{2,1,0:T(8,128)S(1)} %get-tuple-element.180), channel_id=1, source_target_pairs={{0,1},{1,2},{2,3},{3,4},{4,5},{5,6},{6,7},{8,9},{9,10},{10,11},{11... | collective-permute-start | bytes 4760 | tf_op jit(solution)/shard_map/while/body/eval_jaxpr/ppermute | solution.py:16
  928.9 24.8 %all-to-all-start = ((f32[64,1,192]{2,1,0:T(1,128)}), f32[64,1,192]{2,1,0:T(1,128)S(1)}, u32[]{:S(2)}, u32[]{:S(2)}) async-start(f32[64,1,192]{2,1,0:T(1,128)} %reshape.136), calls=%async_computation | async-start | bytes 131072 | tf_op jit(solution)/shard_map/while/body/eval_jaxpr/all_to_all | solution.py:42
  947.1 29.1 %collective-permute-start.2 = (f32[6,66,1]{2,1,0:T(8,128)S(1)}, f32[6,66,1]{2,1,0:T(8,128)S(1)}, u32[]{:S(2)}, u32[]{:S(2)}) collective-permute-start(f32[6,66,1]{2,1,0:T(8,128)S(1)} %get-tuple-element.180), channel_id=1, source_target_pairs={{0,1},{1,2},{2,3},{3,4},{4,5},{5,6},{6,7},{8,9},{9,10},{10,11},{11... | collective-permute-start | bytes 4760 | tf_op jit(solution)/shard_map/while/body/eval_jaxpr/ppermute | solution.py:16
  991.6 24.8 %all-to-all-start = ((f32[64,1,192]{2,1,0:T(1,128)}), f32[64,1,192]{2,1,0:T(1,128)S(1)}, u32[]{:S(2)}, u32[]{:S(2)}) async-start(f32[64,1,192]{2,1,0:T(1,128)} %reshape.136), calls=%async_computation | async-start | bytes 131072 | tf_op jit(solution)/shard_map/while/body/eval_jaxpr/all_to_all | solution.py:42
  1009.9 29.1 %collective-permute-start.2 = (f32[6,66,1]{2,1,0:T(8,128)S(1)}, f32[6,66,1]{2,1,0:T(8,128)S(1)}, u32[]{:S(2)}, u32[]{:S(2)}) collective-permute-start(f32[6,66,1]{2,1,0:T(8,128)S(1)} %get-tuple-element.180), channel_id=1, source_target_pairs={{0,1},{1,2},{2,3},{3,4},{4,5},{5,6},{6,7},{8,9},{9,10},{10,11},{11... | collective-permute-start | bytes 4760 | tf_op jit(solution)/shard_map/while/body/eval_jaxpr/ppermute | solution.py:16
  1054.3 24.8 %all-to-all-start = ((f32[64,1,192]{2,1,0:T(1,128)}), f32[64,1,192]{2,1,0:T(1,128)S(1)}, u32[]{:S(2)}, u32[]{:S(2)}) async-start(f32[64,1,192]{2,1,0:T(1,128)} %reshape.136), calls=%async_computation | async-start | bytes 131072 | tf_op jit(solution)/shard_map/while/body/eval_jaxpr/all_to_all | solution.py:42
  1072.6 29.1 %collective-permute-start.2 = (f32[6,66,1]{2,1,0:T(8,128)S(1)}, f32[6,66,1]{2,1,0:T(8,128)S(1)}, u32[]{:S(2)}, u32[]{:S(2)}) collective-permute-start(f32[6,66,1]{2,1,0:T(8,128)S(1)} %get-tuple-element.180), channel_id=1, source_target_pairs={{0,1},{1,2},{2,3},{3,4},{4,5},{5,6},{6,7},{8,9},{9,10},{10,11},{11... | collective-permute-start | bytes 4760 | tf_op jit(solution)/shard_map/while/body/eval_jaxpr/ppermute | solution.py:16
  1117.1 24.8 %all-to-all-start = ((f32[64,1,192]{2,1,0:T(1,128)}), f32[64,1,192]{2,1,0:T(1,128)S(1)}, u32[]{:S(2)}, u32[]{:S(2)}) async-start(f32[64,1,192]{2,1,0:T(1,128)} %reshape.136), calls=%async_computation | async-start | bytes 131072 | tf_op jit(solution)/shard_map/while/body/eval_jaxpr/all_to_all | solution.py:42
  1135.3 29.1 %collective-permute-start.2 = (f32[6,66,1]{2,1,0:T(8,128)S(1)}, f32[6,66,1]{2,1,0:T(8,128)S(1)}, u32[]{:S(2)}, u32[]{:S(2)}) collective-permute-start(f32[6,66,1]{2,1,0:T(8,128)S(1)} %get-tuple-element.180), channel_id=1, source_target_pairs={{0,1},{1,2},{2,3},{3,4},{4,5},{5,6},{6,7},{8,9},{9,10},{10,11},{11... | collective-permute-start | bytes 4760 | tf_op jit(solution)/shard_map/while/body/eval_jaxpr/ppermute | solution.py:16
  1179.8 24.8 %all-to-all-start = ((f32[64,1,192]{2,1,0:T(1,128)}), f32[64,1,192]{2,1,0:T(1,128)S(1)}, u32[]{:S(2)}, u32[]{:S(2)}) async-start(f32[64,1,192]{2,1,0:T(1,128)} %reshape.136), calls=%async_computation | async-start | bytes 131072 | tf_op jit(solution)/shard_map/while/body/eval_jaxpr/all_to_all | solution.py:42
  1198.1 29.1 %collective-permute-start.2 = (f32[6,66,1]{2,1,0:T(8,128)S(1)}, f32[6,66,1]{2,1,0:T(8,128)S(1)}, u32[]{:S(2)}, u32[]{:S(2)}) collective-permute-start(f32[6,66,1]{2,1,0:T(8,128)S(1)} %get-tuple-element.180), channel_id=1, source_target_pairs={{0,1},{1,2},{2,3},{3,4},{4,5},{5,6},{6,7},{8,9},{9,10},{10,11},{11... | collective-permute-start | bytes 4760 | tf_op jit(solution)/shard_map/while/body/eval_jaxpr/ppermute | solution.py:16
  1242.6 24.8 %all-to-all-start = ((f32[64,1,192]{2,1,0:T(1,128)}), f32[64,1,192]{2,1,0:T(1,128)S(1)}, u32[]{:S(2)}, u32[]{:S(2)}) async-start(f32[64,1,192]{2,1,0:T(1,128)} %reshape.136), calls=%async_computation | async-start | bytes 131072 | tf_op jit(solution)/shard_map/while/body/eval_jaxpr/all_to_all | solution.py:42
  1260.8 29.1 %collective-permute-start.2 = (f32[6,66,1]{2,1,0:T(8,128)S(1)}, f32[6,66,1]{2,1,0:T(8,128)S(1)}, u32[]{:S(2)}, u32[]{:S(2)}) collective-permute-start(f32[6,66,1]{2,1,0:T(8,128)S(1)} %get-tuple-element.180), channel_id=1, source_target_pairs={{0,1},{1,2},{2,3},{3,4},{4,5},{5,6},{6,7},{8,9},{9,10},{10,11},{11... | collective-permute-start | bytes 4760 | tf_op jit(solution)/shard_map/while/body/eval_jaxpr/ppermute | solution.py:16
  (143 other events, 2537.6 us)
